TPU v7x, 256 devices: a whole 4x4x8 slice. The times are simulated.
256 devices in a mesh: space: 32 (over x, z_hi, y), vel: 8 (over z_lo, core).
Axes of the slice: x: 4, y: 4, z: 8 (z_hi: 2, z_lo: 4; z = z_hi * 4 + z_lo), core: 2. Of those that a mesh axis runs over, the one named last changes fastest.
Arguments:
- distribution: float32 [64, 128, 4096], P('space', None, 'vel'), may hold values from 0.05 to 1
- cell_flags: int32 [64, 128], P('space'), may hold values from 0 to 3, as said below
- kernel_alpha: float32 [8, 4096], replicated, may hold values from -1 to 1, as said below
- kernel_beta: float32 [8, 4096], replicated, may hold values from -1 to 1, as said below
- kernel_loss: float32 [4096], replicated, may hold values from 0 to 1, as said below
- boundary_states: float32 [2, 4096], replicated, may hold values from 0.05 to 1
Outputs:
- updated: float32 [64, 128, 4096], P('space', None, 'vel')
Inputs may be any that keep to these rules, and one draw needn't show every extreme that they name: `cell_flags`: 0 marks a fluid cell, 1 a wall cell, 2 an inflow cell, 3 an outflow cell; every type occurs. `kernel_alpha`: even in the mode: the entry of mode (k1, k2, k3) equals that of mode (-k1, -k2, -k3) modulo 16, for every direction. `kernel_beta`: even in the mode, as kernel_alpha. `kernel_loss`: even in the mode, as kernel_alpha.
All inputs are finite; a program needn't handle non-finite values.
Results may differ from a plain program's by a relative error of at most 0.0001.
Values sent between devices are 32-bit elements; how exact they have to be, the bound alone decides.
A program may use at most 64 MiB of HBM per device.

v0:
```python
import functools

import jax
import jax.numpy as jnp
import numpy as np
from jax import lax
from jax.experimental import pallas as pl
from jax.experimental.pallas import tpu as pltpu
from jax.sharding import PartitionSpec as P

VG = 16
PLANE = VG * VG
VEL = VG * PLANE
DIRS = 8
FILTERS = 2 * DIRS + 1
PEERS = 8
SLAB = 16
ROWS = 8
CHUNKS = SLAB // ROWS
COLUMN = 4
MESH = pl.DeviceIdType.MESH
f32 = jnp.float32
bf16 = jnp.bfloat16


def half_modes():
    own = [((0, 0), (0, 8)), ((8, 0), (8, 8))]
    seen, pairs = set(), []
    for a in range(VG):
        for b in range(VG):
            twin = ((-a) % VG, (-b) % VG)
            if twin == (a, b) or twin in seen:
                continue
            seen.add((a, b))
            pairs.append((a, b))
    return own, pairs


def tables():
    own, pairs = half_modes()
    j, l = np.meshgrid(np.arange(VG), np.arange(VG), indexing="ij")
    j, l = j.reshape(-1), l.reshape(-1)

    def angle(mode):
        return ((mode[0] * j + mode[1] * l) % VG) * (2.0 * np.pi / VG)

    forward = np.zeros((PLANE, PLANE))
    inverse = np.zeros((PLANE, PLANE))
    pick = np.zeros((PLANE, PLANE))
    half = PLANE // 2
    for lane, (first, second) in enumerate(own):
        forward[:, lane] = np.cos(angle(first))
        forward[:, half + lane] = np.cos(angle(second))
        inverse[lane] = np.cos(angle(first))
        inverse[half + lane] = np.cos(angle(second))
        one, two = (first[0] * VG + first[1], second[0] * VG + second[1])
        pick[one, lane] = pick[two, lane] = 0.5
        pick[one, half + lane], pick[two, half + lane] = 0.5, -0.5
    for lane, mode in enumerate(pairs, start=len(own)):
        forward[:, lane] = np.cos(angle(mode))
        forward[:, half + lane] = -np.sin(angle(mode))
        inverse[lane] = 2.0 * np.cos(angle(mode))
        inverse[half + lane] = -2.0 * np.sin(angle(mode))
        pick[mode[0] * VG + mode[1], lane] = 1.0

    def parts(table):
        high = table.astype(np.float32).astype(bf16)
        low = (table - high.astype(np.float64)).astype(np.float32).astype(bf16)
        return [high, low]

    stack = parts(forward) + parts(inverse / VEL) + [pick.astype(bf16)]
    return np.stack(stack)


def times_root(re, im, power):
    power %= VG
    if power == 0:
        return re, im
    if power == 4:
        return im, -re
    c = float(np.cos(2.0 * np.pi * power / VG))
    s = float(np.sin(2.0 * np.pi * power / VG))
    if power == 2:
        return (re + im) * c, (im - re) * c
    if power == 6:
        return (im - re) * s, (re + im) * (-s)
    return re * c + im * s, im * c - re * s


def four_points(z):
    (ar, ai), (br, bi), (cr, ci), (dr, di) = z
    pr, pi_, mr, mi = ar + cr, ai + ci, ar - cr, ai - ci
    qr, qi, nr, ni = br + dr, bi + di, br - dr, bi - di
    return [(pr + qr, pi_ + qi), (mr + ni, mi - nr), (pr - qr, pi_ - qi), (mr - ni, mi + nr)]


def line_transform(z):
    mid = [four_points([z[4 * a + b] for a in range(4)]) for b in range(4)]
    out = [None] * VG
    for k in range(4):
        group = four_points([times_root(*mid[b][k], b * k) for b in range(4)])
        for m in range(4):
            out[k + 4 * m] = group[m]
    return out


def line_inverse(z):
    flipped = line_transform([(im, re) for re, im in z])
    return [(re, im) for im, re in flipped]


def split_two(x):
    high = x.astype(bf16)
    return high, (x - high.astype(f32)).astype(bf16)


def dot_three(x, high, low):
    x_high, x_low = split_two(x)
    dot = functools.partial(jnp.dot, preferred_element_type=f32)
    return dot(x_high, high) + (dot(x_low, high) + dot(x_high, low))


def flag_column(row, offset):
    lanes = lax.broadcasted_iota(jnp.int32, (ROWS, 128), 1)
    rows = lax.broadcasted_iota(jnp.int32, (ROWS, 128), 0)
    wide = jnp.broadcast_to(row.astype(f32), (ROWS, 128))
    return jnp.sum(jnp.where(lanes == rows + offset, wide, 0.0), axis=1, keepdims=True)


def transport(flags, states, own_ref, left_ref, right_ref, put):
    left, own, right = flags[0:2], flags[2:4], flags[4:6]

    def ghost(val, mark, low, high, edge):
        if edge:
            val = jnp.where(mark == 4.0, 0.0, val)
        return jnp.where(mark == 1.0, low, jnp.where(mark == 2.0, high, val))

    def stencil(g, one, two, a, mark):
        second = (1.0 - 1.5 * a + 0.5 * a * a) * g + (2.0 * a - a * a) * one + (0.5 * a * a - 0.5 * a) * two
        return jnp.where(mark == 0.0, second, jnp.where(mark == 3.0, g - a * (g - one), g))

    def side(v, positive):
        for part in range(2):
            lanes = slice(part * PLANE, (part + 1) * PLANE)
            a = jnp.abs((2 * (2 * v + part) - 15).astype(f32)) * (0.9 / 15.0)
            low, high = states[v, 0, part : part + 1, :], states[v, 1, part : part + 1, :]
            own0 = ghost(own_ref[v, 0, :, lanes], own[0], low, high, False)
            own1 = ghost(own_ref[v, 1, :, lanes], own[1], low, high, False)
            if positive:
                near = ghost(left_ref[v - 4, 1, :, lanes], left[1], low, high, True)
                far = ghost(left_ref[v - 4, 0, :, lanes], left[0], low, high, True)
                put(v, part, stencil(own0, near, far, a, own[0]), stencil(own1, own0, near, a, own[1]))
            else:
                near = ghost(right_ref[v, 0, :, lanes], right[0], low, high, True)
                far = ghost(right_ref[v, 1, :, lanes], right[1], low, high, True)
                put(v, part, stencil(own0, own1, near, a, own[0]), stencil(own1, near, far, a, own[1]))

    @pl.loop(0, 4)
    def _(v):
        side(v, False)

    @pl.loop(4, 8)
    def _(v):
        side(v, True)


def collide(filters, tab, moved, spec, modes, first, second, gain):
    rows = VG * 2 * ROWS
    half = PLANE // 2

    def piece(ref, k, x):
        at = k * 2 * ROWS + x * ROWS
        return ref[at : at + ROWS, 0:half], ref[at : at + ROWS, half:PLANE]

    def put(ref, k, x, val):
        at = k * 2 * ROWS + x * ROWS
        ref[at : at + ROWS, 0:half] = val[0]
        ref[at : at + ROWS, half:PLANE] = val[1]

    spec[...] = dot_three(moved[...], tab[0], tab[1])
    for x in range(2):
        done = line_transform([piece(spec, k, x) for k in range(VG)])
        for k in range(VG):
            put(modes, k, x, done[k])

    def filtered(index, target):
        for x in range(2):
            z = [piece(modes, k, x) for k in range(VG)]
            w = []
            for k in range(VG):
                near, far = filters[index, k, 0], filters[index, k, 1]
                twin = z[-k % VG]
                w.append((near * z[k][0] + far * twin[0], near * z[k][1] - far * twin[1]))
            done = line_inverse(w)
            for k in range(VG):
                put(target, k, x, done[k])

    filtered(2 * DIRS, first)
    loss = dot_three(first[...], tab[2], tab[3])
    gain[...] = -(moved[...] * loss)

    @pl.loop(0, DIRS)
    def _(p):
        filtered(p, first)
        filtered(p + DIRS, second)
        one = dot_three(first[...], tab[2], tab[3])
        two = dot_three(second[...], tab[2], tab[3])
        gain[...] += one * two


def step_kernel(
    column, dist, flags, alpha, beta, loss, states, tab, out,
    recv, left1, right1, coll, left2, right2, done, moved, spec, modes, first, second, gain,
    packed, filters, near_flags, marks,
    in_send, in_recv, out_send, out_recv, halo_send, halo_recv, flag_send, flag_recv,
):
    s, v = lax.axis_index("space"), lax.axis_index("vel")
    total = lax.axis_size("space")

    def upper(at):
        return (at // column) % 2

    def slab_of(at, peer):
        turned = (3 - peer // 2) * 2 + peer % 2
        return peer + upper(at) * (turned - peer)

    def partner(at):
        turned = (3 - v // 2) * 2 + v % 2
        change = (upper(at) + upper(s)) % 2
        return {"space": at, "vel": v + change * (turned - v)}

    right = partner((s + 1) % total)
    left = partner((s + total - 1) % total)
    peers = [(v + d) % PEERS for d in range(1, PEERS)]

    barrier = pltpu.get_barrier_semaphore()
    for w in peers:
        pl.semaphore_signal(barrier, inc=1, device_id={"space": s, "vel": w}, device_id_type=MESH)
    for at in (left, right):
        pl.semaphore_signal(barrier, inc=1, device_id=at, device_id_type=MESH)
    pl.semaphore_wait(barrier, PEERS + 1)

    def remote(src, dst, send, rec, at):
        return pltpu.make_async_remote_copy(
            src_ref=src, dst_ref=dst, send_sem=send, recv_sem=rec, device_id=at, device_id_type=MESH
        )

    def cells(peer, n):
        return pl.ds(pl.multiple_of(slab_of(s, peer) * SLAB + n * ROWS, ROWS), ROWS)

    sent = []
    to_right = remote(flags, near_flags.at[0], flag_send.at[0], flag_recv.at[0], right)
    to_left = remote(flags, near_flags.at[1], flag_send.at[1], flag_recv.at[1], left)
    to_right.start()
    to_left.start()
    for n in range(CHUNKS):
        for d, w in enumerate(peers):
            copy = remote(dist.at[:, cells(w, n), :], recv.at[n, v], in_send.at[n, d], in_recv.at[n, v], {"space": s, "vel": w})
            copy.start()
            sent.append(copy)
        pltpu.make_async_copy(dist.at[:, cells(v, n), :], recv.at[n, v], in_recv.at[n, v]).start()

    for which, ref in enumerate((alpha, beta)):
        table = jnp.concatenate([ref[:, k * PLANE : (k + 1) * PLANE] for k in range(VG)], 0)
        one, rest = table.astype(bf16), table
        total_rows = jnp.zeros((VG * DIRS, PLANE), f32)
        for _ in range(3):
            one = rest.astype(bf16)
            rest = rest - one.astype(f32)
            total_rows = total_rows + jnp.dot(one, tab[4], preferred_element_type=f32)
        packed[which * VG * DIRS : (which + 1) * VG * DIRS, :] = total_rows
    rest = loss[...]
    total_rows = jnp.zeros((VG, PLANE), f32)
    for _ in range(3):
        one = rest.astype(bf16)
        rest = rest - one.astype(f32)
        total_rows = total_rows + jnp.dot(one, tab[4], preferred_element_type=f32)
    packed[2 * VG * DIRS :, :] = total_rows
    for k in range(VG):
        for f in range(FILTERS):
            at = 2 * VG * DIRS + k if f == 2 * DIRS else (f // DIRS) * VG * DIRS + k * DIRS + f % DIRS
            for part in range(2):
                row = packed[at : at + 1, part * 128 : (part + 1) * 128]
                filters[f, k, part] = jnp.broadcast_to(row, (ROWS, 128))

    to_right.wait()
    to_left.wait()
    for n in range(CHUNKS):
        offset = slab_of(s, v) * SLAB + n * ROWS
        for x in range(2):
            lefts = flag_column(near_flags[0, x : x + 1, :], offset)
            rights = flag_column(near_flags[1, x : x + 1, :], offset)
            marks[n, x] = jnp.broadcast_to(jnp.where(s == 0, 4.0, lefts), (ROWS, PLANE))
            marks[n, 2 + x] = jnp.broadcast_to(flag_column(flags[x : x + 1, :], offset), (ROWS, PLANE))
            marks[n, 4 + x] = jnp.broadcast_to(jnp.where(s == total - 1, 4.0, rights), (ROWS, PLANE))

    def exchange(phase, n, src, left_dst, right_dst):
        at = phase * CHUNKS + n
        one = remote(src.at[n, 4:8], left_dst.at[n], halo_send.at[at, 0], halo_recv.at[at, 0], right)
        two = remote(src.at[n, 0:4], right_dst.at[n], halo_send.at[at, 1], halo_recv.at[at, 1], left)
        one.start()
        two.start()
        return [one, two]

    def arrived(n):
        for u in range(PEERS):
            pltpu.make_async_copy(recv.at[n, u], recv.at[n, u], in_recv.at[n, u]).wait()

    def work(n):
        def put_moved(u, part, zero, one):
            at = pl.multiple_of((2 * u + part) * 2 * ROWS, 2 * ROWS)
            moved[pl.ds(at, ROWS), :] = zero
            moved[pl.ds(at + ROWS, ROWS), :] = one

        transport([marks[n, r] for r in range(6)], states, recv.at[n], left1.at[n], right1.at[n], put_moved)
        collide(filters, tab, moved, spec, modes, first, second, gain)
        for k in range(VG):
            for x in range(2):
                at = k * 2 * ROWS + x * ROWS
                lanes = slice((k % 2) * PLANE, (k % 2 + 1) * PLANE)
                coll[n, k // 2, x, :, lanes] = moved[at : at + ROWS, :] + 0.5 * gain[at : at + ROWS, :]

    def finish(n):
        def put_done(u, part, zero, one):
            lanes = slice(part * PLANE, (part + 1) * PLANE)
            done[n, u, 0, :, lanes] = zero
            done[n, u, 1, :, lanes] = one

        transport([marks[n, r] for r in range(6)], states, coll.at[n], left2.at[n], right2.at[n], put_done)
        for d, w in enumerate(peers):
            copy = remote(done.at[n, w], out.at[:, cells(v, n), :], out_send.at[n, d], out_recv.at[n, v], {"space": s, "vel": w})
            copy.start()
            sent.append(copy)
        pltpu.make_async_copy(done.at[n, v], out.at[:, cells(v, n), :], out_recv.at[n, v]).start()

    def settle(copies):
        for copy in copies:
            copy.wait()

    halos1, halos2 = {}, {}
    for n in range(CHUNKS):
        arrived(n)
        halos1[n] = exchange(0, n, recv, left1, right1)
        if n > 0:
            settle(halos2[n - 1])
            finish(n - 1)
        settle(halos1[n])
        work(n)
        halos2[n] = exchange(1, n, coll, left2, right2)
    settle(halos2[CHUNKS - 1])
    finish(CHUNKS - 1)
    for copy in sent:
        copy.wait_send()
    for n in range(CHUNKS):
        for u in range(PEERS):
            pltpu.make_async_copy(done.at[n, u], out.at[:, cells(u, n), :], out_recv.at[n, u]).wait()


def build(column, distribution, cell_flags, kernel_alpha, kernel_beta, kernel_loss, boundary_states):
    dims = (CHUNKS, PEERS, 2, ROWS, 2 * PLANE)
    side = (CHUNKS, PEERS // 2, 2, ROWS, 2 * PLANE)
    block = (VG * 2 * ROWS, PLANE)
    vmem = pl.BlockSpec(memory_space=pltpu.VMEM)
    anywhere = pl.BlockSpec(memory_space=pl.ANY)
    dma = pltpu.SemaphoreType.DMA
    states = boundary_states.reshape(2, PEERS, 2, PLANE).transpose(1, 0, 2, 3)
    return pl.pallas_call(
        functools.partial(step_kernel, column),
        out_shape=jax.ShapeDtypeStruct(distribution.shape, f32),
        in_specs=[anywhere] + [vmem] * 6,
        out_specs=anywhere,
        scratch_shapes=[
            pltpu.VMEM(dims, f32),
            pltpu.VMEM(side, f32),
            pltpu.VMEM(side, f32),
            pltpu.VMEM(dims, f32),
            pltpu.VMEM(side, f32),
            pltpu.VMEM(side, f32),
            pltpu.VMEM(dims, f32),
        ]
        + [pltpu.VMEM(block, f32)] * 6
        + [
            pltpu.VMEM((FILTERS * VG, PLANE), f32),
            pltpu.VMEM((FILTERS, VG, 2, ROWS, 128), f32),
            pltpu.VMEM((2, 2, 128), jnp.int32),
            pltpu.VMEM((CHUNKS, 6, ROWS, PLANE), f32),
            dma((CHUNKS, PEERS)),
            dma((CHUNKS, PEERS)),
            dma((CHUNKS, PEERS)),
            dma((CHUNKS, PEERS)),
            dma((2 * CHUNKS, 2)),
            dma((2 * CHUNKS, 2)),
            dma((2,)),
            dma((2,)),
        ],
        compiler_params=pltpu.CompilerParams(
            collective_id=0, has_side_effects=True, vmem_limit_bytes=48 * 1024 * 1024
        ),
    )(distribution, cell_flags, kernel_alpha, kernel_beta, kernel_loss.reshape(VG, PLANE), states, jnp.asarray(tables()))


def solution(mesh, column=COLUMN):
    return jax.shard_map(
        functools.partial(build, column),
        mesh=mesh,
        in_specs=(P("space", None, "vel"), P("space", None), P(), P(), P(), P()),
        out_specs=P("space", None, "vel"),
        check_vma=False,
    )
```

profile of v0, /device:TPU:1, one launch (start us, length us, event | category | flops | bytes accessed | tf_op | source)
XLA Modules:
  0.0 71.3 jit_solution(13484586177382431831)
XLA Ops:
  0.0 0.0 copy-start.5
  0.0 0.0 copy-start.2
  0.0 0.8 %reshape.6.loss = f32[16,256]{1,0:T(8,128)S(1)} reshape(f32[4096]{0:T(1024)} %param.11) | data formatting | bytes 32768 | tf_op jit(solution)/shard_map/reshape | solution.py:399
  0.8 0.0 copy-done.5
  0.8 0.0 copy-start.4
  0.8 0.1 copy-done.2
  0.9 0.6 copy-done.4
  1.5 0.0 copy-start
  1.5 1.1 %copy-done = bf16[5,256,256]{2,1,0:T(8,128)(2,1)S(1)} copy-done((bf16[5,256,256]{2,1,0:T(8,128)(2,1)S(1)}, bf16[5,256,256]{2,1,0:T(8,128)(2,1)}, u32[]{:S(2)}) %copy-start) | copy-done | bytes 655384
  2.6 0.0 copy-start.1
  2.6 1.0 %copy-done.1 = f32[2,128,512]{2,1,0:T(8,128)S(1)} copy-done((f32[2,128,512]{2,1,0:T(8,128)S(1)}, f32[2,128,512]{2,1,0:T(8,128)}, u32[]{:S(2)}) %copy-start.1) | copy-done | bytes 524312
  3.7 0.0 copy-start.3
  3.7 0.9 %copy-done.3 = f32[8,4096]{1,0:T(8,128)S(1)} copy-done((f32[8,4096]{1,0:T(8,128)S(1)}, f32[8,4096]{1,0:T(8,128)}, u32[]{:S(2)}) %copy-start.3) | copy-done | bytes 131096
  4.6 65.9 %shard_map.73 = f32[2,128,512]{2,1,0:T(8,128)S(1)} custom-call(f32[2,128,512]{2,1,0:T(8,128)S(1)} %copy-done.1, s32[2,128]{1,0:T(2,128)S(1)} %copy-done.4, f32[8,4096]{1,0:T(8,128)S(1)} %copy-done.2, f32[8,4096]{1,0:T(8,128)S(1)} %copy-done.3, f32[16,256]{1,0:T(8,128)S(1)} %reshape.6.loss, f32[8,2,2,256]{3,2,1,0:T(2,128)S(1)} %bitcast.3, ...), custom_call_target="tpu_custom_call" | custom-call | tf_op jit(solution)/shard_map/pallas_call | solution.py:367
  70.5 0.8 %copy.12 = f32[2,128,512]{2,1,0:T(8,128)} copy(f32[2,128,512]{2,1,0:T(8,128)S(1)} %shard_map.73) | data formatting | bytes 1048576
  (2 shorter events, 0.0 us)
Async XLA Ops:
  0.0 0.8 %copy-start.5 = (f32[2,4096]{1,0:T(2,128)S(1)}, f32[2,4096]{1,0:T(2,128)}, u32[]{:S(2)}) copy-start(f32[2,4096]{1,0:T(2,128)} %param.12) | copy-start | bytes 98308
  0.0 0.9 %copy-start.2 = (f32[8,4096]{1,0:T(8,128)S(1)}, f32[8,4096]{1,0:T(8,128)}, u32[]{:S(2)}) copy-start(f32[8,4096]{1,0:T(8,128)} %alpha.1) | copy-start | bytes 393220
  0.8 0.7 copy-start.4
  1.5 1.1 %copy-start = (bf16[5,256,256]{2,1,0:T(8,128)(2,1)S(1)}, bf16[5,256,256]{2,1,0:T(8,128)(2,1)}, u32[]{:S(2)}) copy-start(bf16[5,256,256]{2,1,0:T(8,128)(2,1)} %constant.2.clone.tab) | copy-start | bytes 1966084
  2.6 1.0 %copy-start.1 = (f32[2,128,512]{2,1,0:T(8,128)S(1)}, f32[2,128,512]{2,1,0:T(8,128)}, u32[]{:S(2)}) copy-start(f32[2,128,512]{2,1,0:T(8,128)} %dist.1) | copy-start | bytes 1572868
  3.7 0.9 %copy-start.3 = (f32[8,4096]{1,0:T(8,128)S(1)}, f32[8,4096]{1,0:T(8,128)}, u32[]{:S(2)}) copy-start(f32[8,4096]{1,0:T(8,128)} %beta.1) | copy-start | bytes 393220
where the time goes:
time: 71.5 us; the launch traced here: 71.3 us
  Pallas kernels  65.9 us (92%)
  local copies, waits for them, and re-layouts  5.33 us (7%)
    pallas_call x1, Pallas kernels, build(): pl.pallas_call(functools.partial(step_kernel, column), out_shape=jax.Shap...  65.9 us
    unnamed x13, local copies, waits for them, and re-layouts  4.52 us

commit v1 on v0

v1 whole, which is shorter than its diff:
```python
import functools

import jax
import jax.numpy as jnp
import numpy as np
from jax import lax
from jax.experimental import pallas as pl
from jax.experimental.pallas import tpu as pltpu
from jax.sharding import PartitionSpec as P

VG = 16
PLANE = VG * VG
VEL = VG * PLANE
DIRS = 8
FILTERS = 2 * DIRS + 1
PEERS = 8
TURNS = 4
GROUP = TURNS * PEERS
ROWS = 8
CHUNKS = 2
MESH = pl.DeviceIdType.MESH
f32 = jnp.float32
bf16 = jnp.bfloat16


def half_modes():
    own = [((0, 0), (0, 8)), ((8, 0), (8, 8))]
    seen, pairs = set(), []
    for a in range(VG):
        for b in range(VG):
            twin = ((-a) % VG, (-b) % VG)
            if twin == (a, b) or twin in seen:
                continue
            seen.add((a, b))
            pairs.append((a, b))
    return own, pairs


def tables():
    own, pairs = half_modes()
    j, l = np.meshgrid(np.arange(VG), np.arange(VG), indexing="ij")
    j, l = j.reshape(-1), l.reshape(-1)

    def angle(mode):
        return ((mode[0] * j + mode[1] * l) % VG) * (2.0 * np.pi / VG)

    forward = np.zeros((PLANE, PLANE))
    inverse = np.zeros((PLANE, PLANE))
    pick = np.zeros((PLANE, PLANE))
    half = PLANE // 2
    for lane, (first, second) in enumerate(own):
        forward[:, lane] = np.cos(angle(first))
        forward[:, half + lane] = np.cos(angle(second))
        inverse[lane] = np.cos(angle(first))
        inverse[half + lane] = np.cos(angle(second))
        one, two = (first[0] * VG + first[1], second[0] * VG + second[1])
        pick[one, lane] = pick[two, lane] = 0.5
        pick[one, half + lane], pick[two, half + lane] = 0.5, -0.5
    for lane, mode in enumerate(pairs, start=len(own)):
        forward[:, lane] = np.cos(angle(mode))
        forward[:, half + lane] = -np.sin(angle(mode))
        inverse[lane] = 2.0 * np.cos(angle(mode))
        inverse[half + lane] = -2.0 * np.sin(angle(mode))
        pick[mode[0] * VG + mode[1], lane] = 1.0

    def parts(table):
        high = table.astype(np.float32).astype(bf16)
        low = (table - high.astype(np.float64)).astype(np.float32).astype(bf16)
        return [high, low]

    stack = parts(forward) + parts(inverse / VEL) + [pick.astype(bf16)]
    return np.stack(stack)


def times_root(re, im, power):
    power %= VG
    if power == 0:
        return re, im
    if power == 4:
        return im, -re
    c = float(np.cos(2.0 * np.pi * power / VG))
    s = float(np.sin(2.0 * np.pi * power / VG))
    if power == 2:
        return (re + im) * c, (im - re) * c
    if power == 6:
        return (im - re) * s, (re + im) * (-s)
    return re * c + im * s, im * c - re * s


def four_points(z):
    (ar, ai), (br, bi), (cr, ci), (dr, di) = z
    pr, pi_, mr, mi = ar + cr, ai + ci, ar - cr, ai - ci
    qr, qi, nr, ni = br + dr, bi + di, br - dr, bi - di
    return [(pr + qr, pi_ + qi), (mr + ni, mi - nr), (pr - qr, pi_ - qi), (mr - ni, mi + nr)]


def line_transform(z):
    mid = [four_points([z[4 * a + b] for a in range(4)]) for b in range(4)]
    out = [None] * VG
    for k in range(4):
        group = four_points([times_root(*mid[b][k], b * k) for b in range(4)])
        for m in range(4):
            out[k + 4 * m] = group[m]
    return out


def line_inverse(z):
    flipped = line_transform([(im, re) for re, im in z])
    return [(re, im) for im, re in flipped]


def split_two(x):
    high = x.astype(bf16)
    return high, (x - high.astype(f32)).astype(bf16)


def dot_three(x, high, low):
    x_high, x_low = split_two(x)
    dot = functools.partial(jnp.dot, preferred_element_type=f32)
    return dot(x_high, high) + (dot(x_low, high) + dot(x_high, low))


def row_ids(width):
    return lax.broadcasted_iota(jnp.int32, (ROWS, width), 0)


def roll(x, shift):
    return pltpu.roll(x, shift, 0)


def swap_halves(a, b):
    low = row_ids(a.shape[1]) < 4
    return jnp.where(low, a, roll(b, 4)), jnp.where(low, roll(a, 4), b)


def swap_pairs(a, b):
    low = row_ids(a.shape[1]) % 4 < 2
    return jnp.where(low, a, roll(b, 2)), jnp.where(low, roll(a, 6), b)


def turn_groups(tiles):
    a, b, c, d = tiles
    a, c = swap_halves(a, c)
    b, d = swap_halves(b, d)
    a, b = swap_pairs(a, b)
    c, d = swap_pairs(c, d)
    return [a, b, c, d]


def flag_tile(rows, offset):
    lanes = lax.broadcasted_iota(jnp.int32, (ROWS, 128), 1)
    ids = row_ids(128)
    wide = jnp.zeros((ROWS, 128), f32)
    for at, row in enumerate(rows):
        if row is not None:
            wide = jnp.where(ids // 2 == at, jnp.broadcast_to(row.astype(f32), (ROWS, 128)), wide)
    return jnp.sum(jnp.where(lanes == ids % 2 + offset, wide, 0.0), axis=1, keepdims=True)


def ghost(val, mark, low, high):
    return jnp.where(mark == 1.0, low, jnp.where(mark == 2.0, high, val))


def stencil(g, one, two, a, mark):
    second = (1.0 - 1.5 * a + 0.5 * a * a) * g + (2.0 * a - a * a) * one + (0.5 * a * a - 0.5 * a) * two
    return jnp.where(mark == 0.0, second, jnp.where(mark == 3.0, g - a * (g - one), g))


def transport(marks, states, tiles_of, halo_of, put, outer, inner):
    edge, mid = marks(1), marks(2)
    ids = row_ids(PLANE)

    def side(v, positive):
        tiles = tiles_of(v)
        outs = []
        for part in range(2):
            at = pl.ds(pl.multiple_of((2 * v + part) * PLANE, PLANE), PLANE)
            low, high = states[0:1, at], states[1:2, at]
            a = jnp.abs((2 * (2 * v + part) - 15).astype(f32)) * (0.9 / 15.0)
            e = ghost(tiles[part][0], edge, low, high)
            m = ghost(tiles[part][1], mid, low, high)
            new_e, new_m = None, None
            if inner:
                if positive:
                    one = jnp.where(ids < 2, roll(e, 6), roll(m, 2))
                    two = jnp.where(ids < 4, e, roll(m, 4))
                else:
                    one = jnp.where(ids < 6, roll(m, 6), roll(e, 2))
                    two = jnp.where(ids < 4, roll(m, 4), e)
                new_m = stencil(m, one, two, a, mid)
            if outer:
                if halo_of is None:
                    two = m
                else:
                    halo = halo_of(v, positive)
                    if positive == (part == 1):
                        halo = roll(halo, 4)
                    mark = marks(0) if positive else marks(3)
                    halo = ghost(jnp.where(mark == 4.0, 0.0, halo), mark, low, high)
                    two = jnp.where((ids < 4) == positive, halo, m)
                if positive:
                    one = jnp.where(ids % 4 < 2, roll(two, 6), roll(e, 2))
                else:
                    one = jnp.where(ids % 4 < 2, roll(e, 6), roll(two, 2))
                new_e = stencil(e, one, two, a, edge)
            outs.append((new_e, new_m))
        put(v, positive, outs)

    @pl.loop(0, 4)
    def _(v):
        side(v, False)

    @pl.loop(4, 8)
    def _(v):
        side(v, True)


def collide(filters, tab, moved, spec, modes, first, second, gain):
    half = PLANE // 2
    rows = VG * ROWS

    def piece(ref, k, base=0):
        at = base + k * ROWS
        return ref[at : at + ROWS, 0:half], ref[at : at + ROWS, half:PLANE]

    def put(ref, k, val, base=0):
        at = base + k * ROWS
        ref[at : at + ROWS, 0:half] = val[0]
        ref[at : at + ROWS, half:PLANE] = val[1]

    spec[...] = dot_three(moved[...], tab[0], tab[1])
    done = line_transform([piece(spec, k) for k in range(VG)])
    for k in range(VG):
        put(modes, k, done[k])

    def filtered(index, target, base):
        z = [piece(modes, k) for k in range(VG)]
        w = []
        for k in range(VG):
            near, far = filters[index, k, 0], filters[index, k, 1]
            twin = z[-k % VG]
            w.append((near * z[k][0] + far * twin[0], near * z[k][1] - far * twin[1]))
        done = line_inverse(w)
        for k in range(VG):
            put(target, k, done[k], base)

    def both(p, target):
        filtered(p, target, 0)
        filtered(p + DIRS, target, rows)

    def product(source):
        got = dot_three(source[...], tab[2], tab[3])
        return got[0:rows] * got[rows:]

    filtered(2 * DIRS, second, 0)
    both(0, first)
    loss = dot_three(second[0:rows, :], tab[2], tab[3])
    gain[...] = -(moved[...] * loss)

    @pl.loop(0, DIRS // 2 - 1)
    def _(h):
        both(2 * h + 1, second)
        gain[...] += product(first)
        both(2 * h + 2, first)
        gain[...] += product(second)

    both(DIRS - 1, second)
    gain[...] += product(first)
    gain[...] += product(second)


def step_kernel(
    dist_in, flags_in, alpha_in, beta_in, loss_in, states_in, tab_in, out,
    dist, flags, alpha, beta, loss, states, tab, load_sem,
    pack_in, recv, left1, right1, coll, edge_out, left2, right2, pack_out, back, result,
    moved, spec, modes, first, second, gain, packed, filters, near, edge, marks,
    in_send, in_recv, out_send, out_recv, halo_send, halo_recv, flag_send, flag_recv, own_sem,
):
    s, v = lax.axis_index("space"), lax.axis_index("vel")
    total = lax.axis_size("space")
    group, turn = s // TURNS, s % TURNS
    upper = group % 2
    me = turn * PEERS + v

    def mirror(peer):
        return (3 - peer // 2) * 2 + peer % 2

    def block_of(t, peer):
        return (peer + upper * (mirror(peer) - peer)) * TURNS + t

    def peer_at(q):
        return {"space": group * TURNS + q // PEERS, "vel": q % PEERS}

    right = {"space": (s + TURNS) % total, "vel": mirror(v)}
    left = {"space": (s + total - TURNS) % total, "vel": mirror(v)}
    mine = block_of(turn, v)

    loads = [
        pltpu.make_async_copy(src, dst, load_sem.at[i])
        for i, (src, dst) in enumerate(
            [(dist_in, dist), (flags_in, flags), (alpha_in, alpha), (beta_in, beta), (loss_in, loss), (states_in, states), (tab_in, tab)]
        )
    ]
    for copy in loads:
        copy.start()
    barrier = pltpu.get_barrier_semaphore()

    @pl.loop(1, GROUP)
    def _(d):
        pl.semaphore_signal(barrier, inc=1, device_id=peer_at((me + d) % GROUP), device_id_type=MESH)

    for at in (left, right):
        pl.semaphore_signal(barrier, inc=1, device_id=at, device_id_type=MESH)

    loads[0].wait()

    @pl.loop(0, GROUP // 2)
    def _(b):
        at = pl.ds(pl.multiple_of(b * ROWS, ROWS), ROWS)
        turned = turn_groups([dist[x, at, part * PLANE : (part + 1) * PLANE] for part in range(2) for x in range(2)])
        for j in range(4):
            pack_in[j % 2, 2 * b + j // 2] = turned[j]

    for copy in loads[1:]:
        copy.wait()
    pl.semaphore_wait(barrier, GROUP + 1)

    def remote(src, dst, send, rec, at):
        return pltpu.make_async_remote_copy(
            src_ref=src, dst_ref=dst, send_sem=send, recv_sem=rec, device_id=at, device_id_type=MESH
        )

    for d in range(1, TURNS):
        at = {"space": group * TURNS + (turn + d) % TURNS, "vel": v}
        remote(flags, near.at[turn], flag_send.at[0], flag_recv.at[0], at).start()
    pltpu.make_async_copy(flags, near.at[turn], flag_recv.at[0]).start()

    for n in range(CHUNKS):

        @pl.loop(1, GROUP)
        def _(d):
            q = (me + d) % GROUP
            src = pack_in.at[n, block_of(q // PEERS, q % PEERS)]
            remote(src, recv.at[n, turn, v], in_send.at[n], in_recv.at[n], peer_at(q)).start()

        pltpu.make_async_copy(pack_in.at[n, mine], recv.at[n, turn, v], in_recv.at[n]).start()

    def pick(rest):
        got = jnp.zeros(rest.shape, f32)
        for _ in range(3):
            one = rest.astype(bf16)
            rest = rest - one.astype(f32)
            got = got + jnp.dot(one, tab[4], preferred_element_type=f32)
        return got

    def by_line(ref):
        return jnp.concatenate([ref[:, k * PLANE : (k + 1) * PLANE] for k in range(VG)], 0)

    packed[0 : VG * DIRS, :] = pick(by_line(alpha))
    packed[VG * DIRS : 2 * VG * DIRS, :] = pick(by_line(beta))
    packed[2 * VG * DIRS :, :] = pick(by_line(loss))
    for k in range(VG):
        for f in range(FILTERS):
            at = 2 * VG * DIRS + k if f == 2 * DIRS else (f // DIRS) * VG * DIRS + k * DIRS + f % DIRS
            for part in range(2):
                row = packed[at : at + 1, part * 128 : (part + 1) * 128]
                filters[f, k, part] = jnp.broadcast_to(row, (ROWS, 128))

    pltpu.make_async_copy(near, near, flag_recv.at[0]).wait()
    edges = [
        remote(near.at[3], edge.at[0], flag_send.at[1], flag_recv.at[1], right),
        remote(near.at[0], edge.at[1], flag_send.at[2], flag_recv.at[2], left),
    ]
    for copy in edges:
        copy.start()
    offset = mine * 4
    for n in range(CHUNKS):
        for at, pair in ((1, (0, 3)), (2, (1, 2))):
            rows = [near[pair[r // 2], r % 2 : r % 2 + 1, :] for r in range(4)]
            marks[n, at] = jnp.broadcast_to(flag_tile(rows, offset + 2 * n), (ROWS, PLANE))

    def exchange(at, ups, downs, ups_dst, downs_dst):
        one = remote(ups, ups_dst, halo_send.at[at, 0], halo_recv.at[at, 0], right)
        two = remote(downs, downs_dst, halo_send.at[at, 1], halo_recv.at[at, 1], left)
        one.start()
        two.start()
        return [one, two]

    def settle(copies):
        for copy in copies:
            copy.wait()

    def begin(n):
        pltpu.make_async_copy(recv.at[n], recv.at[n], in_recv.at[n]).wait()
        return exchange(n, recv.at[n, 3, 4:8], recv.at[n, 0, 0:4], left1.at[n], right1.at[n])

    def work(n, which):
        def tiles_of(u):
            one = swap_halves(recv[n, 0, u], recv[n, 3, u])
            two = swap_halves(recv[n, 1, u], recv[n, 2, u])
            return [(one[part], two[part]) for part in range(2)]

        def halo_of(u, positive):
            return left1[n, u - 4] if positive else right1[n, u]

        def put_moved(u, positive, outs):
            for part in range(2):
                at = pl.multiple_of((2 * u + part) * ROWS, ROWS)
                moved[pl.ds(at, ROWS), :] = outs[part][which]

        transport(lambda r: marks[n, r], states, tiles_of, halo_of, put_moved, which == 0, which == 1)
        collide(filters, tab, moved, spec, modes, first, second, gain)
        for u in range(PEERS):
            pair = []
            for part in range(2):
                at = (2 * u + part) * ROWS
                pair.append(moved[at : at + ROWS, :] + 0.5 * gain[at : at + ROWS, :])
                coll[n, u, part, which] = pair[part]
            if which == 0 and u < 4:
                edge_out[n, 1, u] = swap_halves(*pair)[0]
            if which == 0 and u >= 4:
                edge_out[n, 0, u - 4] = swap_halves(*pair)[1]

    def pass_on(n):
        return exchange(CHUNKS + n, edge_out.at[n, 0], edge_out.at[n, 1], left2.at[n], right2.at[n])

    def give(n, t, u):
        q = t * PEERS + u

        @pl.when(q != me)
        def _():
            remote(pack_out.at[n, t, u], back.at[n, mine], out_send.at[n], out_recv.at[n], peer_at(q)).start()

        @pl.when(q == me)
        def _():
            pltpu.make_async_copy(pack_out.at[n, t, u], back.at[n, mine], out_recv.at[n]).start()

    def collided(n):
        def tiles_of(u):
            return [(coll[n, u, part, 0], coll[n, u, part, 1]) for part in range(2)]

        return tiles_of

    def finish_most(n):
        def put_done(u, positive, outs):
            one, two = swap_halves(outs[0][1], outs[1][1])
            pack_out[n, 1, u] = one
            pack_out[n, 2, u] = two
            ends = swap_halves(outs[0][0], outs[1][0])
            if positive:
                pack_out[n, 3, u] = ends[1]
            else:
                pack_out[n, 0, u] = ends[0]

        transport(lambda r: marks[n, r], states, collided(n), None, put_done, True, True)

        @pl.loop(0, 3 * PEERS)
        def _(d):
            u = (v + 1 + d) % PEERS
            give(n, (turn + d // PEERS) % 3 + u // 4, u)

    def finish_rest(n):
        def halo_of(u, positive):
            return left2[n, u - 4] if positive else right2[n, u]

        def put_done(u, positive, outs):
            ends = swap_halves(outs[0][0], outs[1][0])
            if positive:
                pack_out[n, 0, u] = ends[0]
            else:
                pack_out[n, 3, u] = ends[1]

        transport(lambda r: marks[n, r], states, collided(n), halo_of, put_done, True, False)

        @pl.loop(0, PEERS)
        def _(d):
            u = (v + 1 + d) % PEERS
            give(n, 3 - 3 * (u // 4), u)

    one1 = begin(0)
    work(0, 1)
    settle(edges)
    for n in range(CHUNKS):
        lefts = flag_tile([edge[0, 0:1, :], edge[0, 1:2, :], None, None], offset + 2 * n)
        rights = flag_tile([None, None, edge[1, 0:1, :], edge[1, 1:2, :]], offset + 2 * n)
        marks[n, 0] = jnp.broadcast_to(jnp.where(group == 0, 4.0, lefts), (ROWS, PLANE))
        marks[n, 3] = jnp.broadcast_to(jnp.where(group == total // TURNS - 1, 4.0, rights), (ROWS, PLANE))
    settle(one1)
    work(0, 0)
    one2 = pass_on(0)
    two1 = begin(1)
    finish_most(0)
    work(1, 1)
    settle(one2)
    finish_rest(0)
    settle(two1)
    work(1, 0)
    two2 = pass_on(1)
    finish_most(1)
    settle(two2)
    finish_rest(1)
    for n in range(CHUNKS):
        pltpu.make_async_copy(back.at[n], back.at[n], out_recv.at[n]).wait()

    @pl.loop(0, GROUP // 2)
    def _(b):
        at = pl.ds(pl.multiple_of(b * ROWS, ROWS), ROWS)
        turned = turn_groups([back[j % 2, 2 * b + j // 2] for j in range(4)])
        for part in range(2):
            for x in range(2):
                result[x, at, part * PLANE : (part + 1) * PLANE] = turned[2 * part + x]

    last = pltpu.make_async_copy(result, out, own_sem)
    last.start()
    for n in range(CHUNKS):
        for buf, sem in ((pack_in, in_send), (back, out_send)):
            pltpu.make_async_copy(buf.at[n, 0 : GROUP - 1], buf.at[n, 0 : GROUP - 1], sem.at[n]).wait()
    pltpu.make_async_copy(near.at[0:3], near.at[0:3], flag_send.at[0]).wait()
    last.wait()


def build(distribution, cell_flags, kernel_alpha, kernel_beta, kernel_loss, boundary_states):
    tile = (ROWS, PLANE)
    block = (VG * ROWS, PLANE)
    double = (2 * VG * ROWS, PLANE)
    anywhere = pl.BlockSpec(memory_space=pl.ANY)
    dma = pltpu.SemaphoreType.DMA

    def room(*dims):
        return pltpu.VMEM(dims + tile, f32)

    return pl.pallas_call(
        step_kernel,
        out_shape=jax.ShapeDtypeStruct(distribution.shape, f32),
        in_specs=[anywhere] * 7,
        out_specs=anywhere,
        scratch_shapes=[
            pltpu.VMEM(distribution.shape, f32),
            pltpu.VMEM((2, 128), jnp.int32),
            pltpu.VMEM((DIRS, VEL), f32),
            pltpu.VMEM((DIRS, VEL), f32),
            pltpu.VMEM((1, VEL), f32),
            pltpu.VMEM((2, VEL), f32),
            pltpu.VMEM((5, PLANE, PLANE), bf16),
            dma((7,)),
            room(CHUNKS, GROUP),
            room(CHUNKS, TURNS, PEERS),
            room(CHUNKS, PEERS // 2),
            room(CHUNKS, PEERS // 2),
            room(CHUNKS, PEERS, 2, 2),
            room(CHUNKS, 2, PEERS // 2),
            room(CHUNKS, PEERS // 2),
            room(CHUNKS, PEERS // 2),
            room(CHUNKS, TURNS, PEERS),
            room(CHUNKS, GROUP),
            pltpu.VMEM(distribution.shape, f32),
        ]
        + [pltpu.VMEM(block, f32)] * 3
        + [pltpu.VMEM(double, f32)] * 2
        + [pltpu.VMEM(block, f32)]
        + [
            pltpu.VMEM((FILTERS * VG, PLANE), f32),
            pltpu.VMEM((FILTERS, VG, 2, ROWS, 128), f32),
            pltpu.VMEM((TURNS, 2, 128), jnp.int32),
            pltpu.VMEM((2, 2, 128), jnp.int32),
            room(CHUNKS, 4),
            dma((CHUNKS,)),
            dma((CHUNKS,)),
            dma((CHUNKS,)),
            dma((CHUNKS,)),
            dma((2 * CHUNKS, 2)),
            dma((2 * CHUNKS, 2)),
            dma((3,)),
            dma((3,)),
            dma(()),
        ],
        compiler_params=pltpu.CompilerParams(collective_id=0, has_side_effects=True),
    )(distribution, cell_flags, kernel_alpha, kernel_beta, kernel_loss.reshape(1, VEL), boundary_states, jnp.asarray(tables()))


def solution(mesh):
    return jax.shard_map(
        build,
        mesh=mesh,
        in_specs=(P("space", None, "vel"), P("space", None), P(), P(), P(), P()),
        out_specs=P("space", None, "vel"),
        check_vma=False,
    )
```

time: 71.5 us -> 53.4 us (0.75)
  the two profiles are of different devices: /device:TPU:1 before, /device:TPU:25 now
where the time goes in v1:
time: 53.4 us; the launch traced here: 53.3 us
  Pallas kernels  51.4 us (96%)
  local copies, waits for them, and re-layouts  1.87 us (4%)
    pallas_call x1, Pallas kernels, build(): pl.pallas_call(step_kernel, out_shape=jax.ShapeDtypeStruct(distribution.s...  51.4 us
    unnamed x1, local copies, waits for them, and re-layouts  1.87 us

profile of v1, /device:TPU:25, one launch (start us, length us, event | category | flops | bytes accessed | tf_op | source)
XLA Modules:
  0.0 53.3 jit_solution(11399316822634930824)
XLA Ops:
  0.0 51.4 %shard_map.73 = f32[2,128,512]{2,1,0:T(8,128)} custom-call(f32[2,128,512]{2,1,0:T(8,128)} %dist_in.1, s32[2,128]{1,0:T(2,128)} %flags_in.1, f32[8,4096]{1,0:T(8,128)} %alpha_in.1, f32[8,4096]{1,0:T(8,128)} %beta_in.1, f32[1,4096]{1,0:T(1,128)} %bitcast.1, f32[2,4096]{1,0:T(2,128)} %states_in.1, bf16[5,256,256]{2,1,0:T(8,128)(2,1)} %constant.2.clone.tab_in), custom_call_target="tpu_custom_call" | custom-call | tf_op jit(solution)/shard_map/pallas_call | solution.py:532
  51.4 1.9 %copy.9 = f32[2,128,512]{2,1,0:T(8,128)} copy(f32[2,128,512]{2,1,0:T(8,128)} %shard_map.73) | data formatting | bytes 1048576

commit v2 on v1

--- a/solution.py
+++ b/solution.py
@@ -203,7 +203,7 @@
                 else:
                     one = jnp.where(ids % 4 < 2, roll(e, 6), roll(two, 2))
                 new_e = stencil(e, one, two, a, edge)
-            outs.append((new_e, new_m))
+            outs.append((new_e, new_m, e))
         put(v, positive, outs)
 
     @pl.loop(0, 4)
@@ -272,9 +272,9 @@
 def step_kernel(
     dist_in, flags_in, alpha_in, beta_in, loss_in, states_in, tab_in, out,
     dist, flags, alpha, beta, loss, states, tab, load_sem,
-    pack_in, recv, left1, right1, coll, edge_out, left2, right2, pack_out, back, result,
-    moved, spec, modes, first, second, gain, packed, filters, near, edge, marks,
-    in_send, in_recv, out_send, out_recv, halo_send, halo_recv, flag_send, flag_recv, own_sem,
+    pack_in, recv, left1, right1, coll, pack_far, far, pack_out, back, result,
+    moved, spec, modes, first, second, gain, packed, filters, near, edge, marks, own_marks,
+    in_send, in_recv, out_send, out_recv, far_send, far_recv, halo_send, halo_recv, flag_send, flag_recv, own_sem,
 ):
     s, v = lax.axis_index("space"), lax.axis_index("vel")
     total = lax.axis_size("space")
@@ -283,7 +283,7 @@
     me = turn * PEERS + v
 
     def mirror(peer):
-        return (3 - peer // 2) * 2 + peer % 2
+        return (peer + PEERS // 2) % PEERS
 
     def block_of(t, peer):
         return (peer + upper * (mirror(peer) - peer)) * TURNS + t
@@ -379,6 +379,13 @@
             rows = [near[pair[r // 2], r % 2 : r % 2 + 1, :] for r in range(4)]
             marks[n, at] = jnp.broadcast_to(flag_tile(rows, offset + 2 * n), (ROWS, PLANE))
 
+    for x in range(2):
+        wide = jnp.broadcast_to(flags[x : x + 1, :].astype(f32), (ROWS, 128))
+        lanes = lax.broadcasted_iota(jnp.int32, (ROWS, 128), 1)
+        for b in range(GROUP // 2):
+            column = jnp.sum(jnp.where(lanes == row_ids(128) + b * ROWS, wide, 0.0), axis=1, keepdims=True)
+            own_marks[x, b * ROWS : (b + 1) * ROWS, :] = jnp.broadcast_to(column, (ROWS, 128))
+
     def exchange(at, ups, downs, ups_dst, downs_dst):
         one = remote(ups, ups_dst, halo_send.at[at, 0], halo_recv.at[at, 0], right)
         two = remote(downs, downs_dst, halo_send.at[at, 1], halo_recv.at[at, 1], left)
@@ -416,24 +423,6 @@
                 at = (2 * u + part) * ROWS
                 pair.append(moved[at : at + ROWS, :] + 0.5 * gain[at : at + ROWS, :])
                 coll[n, u, part, which] = pair[part]
-            if which == 0 and u < 4:
-                edge_out[n, 1, u] = swap_halves(*pair)[0]
-            if which == 0 and u >= 4:
-                edge_out[n, 0, u - 4] = swap_halves(*pair)[1]
-
-    def pass_on(n):
-        return exchange(CHUNKS + n, edge_out.at[n, 0], edge_out.at[n, 1], left2.at[n], right2.at[n])
-
-    def give(n, t, u):
-        q = t * PEERS + u
-
-        @pl.when(q != me)
-        def _():
-            remote(pack_out.at[n, t, u], back.at[n, mine], out_send.at[n], out_recv.at[n], peer_at(q)).start()
-
-        @pl.when(q == me)
-        def _():
-            pltpu.make_async_copy(pack_out.at[n, t, u], back.at[n, mine], out_recv.at[n]).start()
 
     def collided(n):
         def tiles_of(u):
@@ -441,41 +430,37 @@
 
         return tiles_of
 
-    def finish_most(n):
+    def finish(n):
         def put_done(u, positive, outs):
             one, two = swap_halves(outs[0][1], outs[1][1])
             pack_out[n, 1, u] = one
             pack_out[n, 2, u] = two
             ends = swap_halves(outs[0][0], outs[1][0])
+            raw = swap_halves(outs[0][2], outs[1][2])
             if positive:
                 pack_out[n, 3, u] = ends[1]
+                pack_out[n, 0, u] = raw[0]
+                pack_far[n, u] = raw[1]
             else:
                 pack_out[n, 0, u] = ends[0]
+                pack_out[n, 3, u] = raw[1]
+                pack_far[n, u] = raw[0]
 
         transport(lambda r: marks[n, r], states, collided(n), None, put_done, True, True)
-
-        @pl.loop(0, 3 * PEERS)
-        def _(d):
-            u = (v + 1 + d) % PEERS
-            give(n, (turn + d // PEERS) % 3 + u // 4, u)
-
-    def finish_rest(n):
-        def halo_of(u, positive):
-            return left2[n, u - 4] if positive else right2[n, u]
-
-        def put_done(u, positive, outs):
-            ends = swap_halves(outs[0][0], outs[1][0])
-            if positive:
-                pack_out[n, 0, u] = ends[0]
-            else:
-                pack_out[n, 3, u] = ends[1]
-
-        transport(lambda r: marks[n, r], states, collided(n), halo_of, put_done, True, False)
 
         @pl.loop(0, PEERS)
         def _(d):
-            u = (v + 1 + d) % PEERS
-            give(n, 3 - 3 * (u // 4), u)
+            u = (v + d) % PEERS
+            at = (s - turn + total + TURNS * (2 * (u // 4) - 1)) % total + 3 * (1 - u // 4)
+            remote(pack_far.at[n, u], far.at[n, mine], far_send.at[n], far_recv.at[n], {"space": at, "vel": u}).start()
+
+        @pl.loop(1, GROUP)
+        def _(d):
+            q = (me + d) % GROUP
+            src = pack_out.at[n, q // PEERS, q % PEERS]
+            remote(src, back.at[n, mine], out_send.at[n], out_recv.at[n], peer_at(q)).start()
+
+        pltpu.make_async_copy(pack_out.at[n, turn, v], back.at[n, mine], out_recv.at[n]).start()
 
     one1 = begin(0)
     work(0, 1)
@@ -487,34 +472,72 @@
         marks[n, 3] = jnp.broadcast_to(jnp.where(group == total // TURNS - 1, 4.0, rights), (ROWS, PLANE))
     settle(one1)
     work(0, 0)
-    one2 = pass_on(0)
     two1 = begin(1)
-    finish_most(0)
+    finish(0)
     work(1, 1)
-    settle(one2)
-    finish_rest(0)
     settle(two1)
     work(1, 0)
-    two2 = pass_on(1)
-    finish_most(1)
-    settle(two2)
-    finish_rest(1)
+    finish(1)
     for n in range(CHUNKS):
         pltpu.make_async_copy(back.at[n], back.at[n], out_recv.at[n]).wait()
-
-    @pl.loop(0, GROUP // 2)
-    def _(b):
+    up_end = jnp.logical_and(turn == 0, v >= PEERS // 2)
+    down_end = jnp.logical_and(turn == TURNS - 1, v < PEERS // 2)
+
+    def unpack(b, fix):
         at = pl.ds(pl.multiple_of(b * ROWS, ROWS), ROWS)
         turned = turn_groups([back[j % 2, 2 * b + j // 2] for j in range(4)])
+        if fix is not None:
+            turned = fix(at, turned, turn_groups([far[j % 2, 2 * b + j // 2] for j in range(4)]))
         for part in range(2):
             for x in range(2):
                 result[x, at, part * PLANE : (part + 1) * PLANE] = turned[2 * part + x]
+
+    def fix_end(keep, order):
+        def fix(at, own, near_by):
+            done = [None] * 4
+            for part in range(2):
+                a = jnp.abs((2 * (2 * v + part) - 15).astype(f32)) * (0.9 / 15.0)
+                first, second = [2 * part + x for x in order]
+                one, two = near_by[second] * keep, near_by[first] * keep
+                mark = [jnp.broadcast_to(own_marks[x, at, 0:1], (ROWS, PLANE)) for x in order]
+                done[first] = stencil(own[first], one, two, a, mark[0])
+                done[second] = stencil(own[second], own[first], one, a, mark[1])
+            return done
+
+        return fix
+
+    @pl.when(up_end)
+    def _():
+        for n in range(CHUNKS):
+            pltpu.make_async_copy(far.at[n], far.at[n], far_recv.at[n]).wait()
+        fix = fix_end(jnp.where(group == 0, 0.0, 1.0), (0, 1))
+
+        @pl.loop(0, GROUP // 2)
+        def _(b):
+            unpack(b, fix)
+
+    @pl.when(down_end)
+    def _():
+        for n in range(CHUNKS):
+            pltpu.make_async_copy(far.at[n], far.at[n], far_recv.at[n]).wait()
+        fix = fix_end(jnp.where(group == total // TURNS - 1, 0.0, 1.0), (1, 0))
+
+        @pl.loop(0, GROUP // 2)
+        def _(b):
+            unpack(b, fix)
+
+    @pl.when(jnp.logical_not(jnp.logical_or(up_end, down_end)))
+    def _():
+        @pl.loop(0, GROUP // 2)
+        def _(b):
+            unpack(b, None)
 
     last = pltpu.make_async_copy(result, out, own_sem)
     last.start()
     for n in range(CHUNKS):
         for buf, sem in ((pack_in, in_send), (back, out_send)):
             pltpu.make_async_copy(buf.at[n, 0 : GROUP - 1], buf.at[n, 0 : GROUP - 1], sem.at[n]).wait()
+        pltpu.make_async_copy(pack_far.at[n], pack_far.at[n], far_send.at[n]).wait()
     pltpu.make_async_copy(near.at[0:3], near.at[0:3], flag_send.at[0]).wait()
     last.wait()
 
@@ -548,9 +571,8 @@
             room(CHUNKS, PEERS // 2),
             room(CHUNKS, PEERS // 2),
             room(CHUNKS, PEERS, 2, 2),
-            room(CHUNKS, 2, PEERS // 2),
-            room(CHUNKS, PEERS // 2),
-            room(CHUNKS, PEERS // 2),
+            room(CHUNKS, PEERS),
+            room(CHUNKS, GROUP),
             room(CHUNKS, TURNS, PEERS),
             room(CHUNKS, GROUP),
             pltpu.VMEM(distribution.shape, f32),
@@ -564,12 +586,15 @@
             pltpu.VMEM((TURNS, 2, 128), jnp.int32),
             pltpu.VMEM((2, 2, 128), jnp.int32),
             room(CHUNKS, 4),
+            pltpu.VMEM((2, 128, 128), f32),
             dma((CHUNKS,)),
             dma((CHUNKS,)),
             dma((CHUNKS,)),
             dma((CHUNKS,)),
-            dma((2 * CHUNKS, 2)),
-            dma((2 * CHUNKS, 2)),
+            dma((CHUNKS,)),
+            dma((CHUNKS,)),
+            dma((CHUNKS, 2)),
+            dma((CHUNKS, 2)),
             dma((3,)),
             dma((3,)),
             dma(()),

time: 53.4 us -> 51.3 us (0.961)
  the two profiles are of different devices: /device:TPU:25 before, /device:TPU:1 now
where the time goes in v2:
time: 51.3 us; the launch traced here: 51.2 us
  Pallas kernels  49.3 us (96%)
  local copies, waits for them, and re-layouts  1.87 us (4%)
    pallas_call x1, Pallas kernels, build(): pl.pallas_call(step_kernel, out_shape=jax.ShapeDtypeStruct(distribution.s...  49.3 us
    unnamed x1, local copies, waits for them, and re-layouts  1.87 us

profile of v2, /device:TPU:1, one launch (start us, length us, event | category | flops | bytes accessed | tf_op | source)
XLA Modules:
  0.0 51.2 jit_solution(1384264913833228814)
XLA Ops:
  0.0 49.3 %shard_map.73 = f32[2,128,512]{2,1,0:T(8,128)} custom-call(f32[2,128,512]{2,1,0:T(8,128)} %dist_in.1, s32[2,128]{1,0:T(2,128)} %flags_in.1, f32[8,4096]{1,0:T(8,128)} %alpha_in.1, f32[8,4096]{1,0:T(8,128)} %beta_in.1, f32[1,4096]{1,0:T(1,128)} %bitcast.1, f32[2,4096]{1,0:T(2,128)} %states_in.1, bf16[5,256,256]{2,1,0:T(8,128)(2,1)} %constant.2.clone.tab_in), custom_call_target="tpu_custom_call" | custom-call | tf_op jit(solution)/shard_map/pallas_call | solution.py:555
  49.3 1.9 %copy.9 = f32[2,128,512]{2,1,0:T(8,128)} copy(f32[2,128,512]{2,1,0:T(8,128)} %shard_map.73) | data formatting | bytes 1048576

commit v3 on v2

--- a/solution.py
+++ b/solution.py
@@ -18,6 +18,7 @@
 GROUP = TURNS * PEERS
 ROWS = 8
 CHUNKS = 2
+GATE_TURN, GATE_PEER = 1, 2
 MESH = pl.DeviceIdType.MESH
 f32 = jnp.float32
 bf16 = jnp.bfloat16
@@ -272,9 +273,9 @@
 def step_kernel(
     dist_in, flags_in, alpha_in, beta_in, loss_in, states_in, tab_in, out,
     dist, flags, alpha, beta, loss, states, tab, load_sem,
-    pack_in, recv, left1, right1, coll, pack_far, far, pack_out, back, result,
+    pack_in, recv, left1, right1, coll, pack_far, far, pack_out, back,
     moved, spec, modes, first, second, gain, packed, filters, near, edge, marks, own_marks,
-    in_send, in_recv, out_send, out_recv, far_send, far_recv, halo_send, halo_recv, flag_send, flag_recv, own_sem,
+    in_send, in_recv, out_send, out_recv, far_send, far_recv, halo_send, halo_recv, flag_send, flag_recv, gate_sem, ready_sem,
 ):
     s, v = lax.axis_index("space"), lax.axis_index("vel")
     total = lax.axis_size("space")
@@ -309,8 +310,16 @@
     def _(d):
         pl.semaphore_signal(barrier, inc=1, device_id=peer_at((me + d) % GROUP), device_id_type=MESH)
 
-    for at in (left, right):
-        pl.semaphore_signal(barrier, inc=1, device_id=at, device_id_type=MESH)
+    gate = jnp.logical_and(turn == GATE_TURN, v == GATE_PEER)
+
+    def next_gate(semaphore):
+        for step in (TURNS, total - TURNS):
+            at = {"space": (s + step) % total, "vel": v}
+            pl.semaphore_signal(semaphore, inc=1, device_id=at, device_id_type=MESH)
+
+    @pl.when(gate)
+    def _():
+        next_gate(barrier)
 
     loads[0].wait()
 
@@ -323,7 +332,7 @@
 
     for copy in loads[1:]:
         copy.wait()
-    pl.semaphore_wait(barrier, GROUP + 1)
+    pl.semaphore_wait(barrier, jnp.where(gate, GROUP + 1, GROUP - 1))
 
     def remote(src, dst, send, rec, at):
         return pltpu.make_async_remote_copy(
@@ -344,6 +353,15 @@
             remote(src, recv.at[n, turn, v], in_send.at[n], in_recv.at[n], peer_at(q)).start()
 
         pltpu.make_async_copy(pack_in.at[n, mine], recv.at[n, turn, v], in_recv.at[n]).start()
+
+    @pl.when(gate)
+    def _():
+        next_gate(gate_sem)
+        pl.semaphore_wait(gate_sem, 2)
+
+        @pl.loop(1, GROUP)
+        def _(d):
+            pl.semaphore_signal(ready_sem, inc=1, device_id=peer_at((me + d) % GROUP), device_id_type=MESH)
 
     def pick(rest):
         got = jnp.zeros(rest.shape, f32)
@@ -367,6 +385,10 @@
                 filters[f, k, part] = jnp.broadcast_to(row, (ROWS, 128))
 
     pltpu.make_async_copy(near, near, flag_recv.at[0]).wait()
+    @pl.when(jnp.logical_not(gate))
+    def _():
+        pl.semaphore_wait(ready_sem, 1)
+
     edges = [
         remote(near.at[3], edge.at[0], flag_send.at[1], flag_recv.at[1], right),
         remote(near.at[0], edge.at[1], flag_send.at[2], flag_recv.at[2], left),
@@ -424,29 +446,55 @@
                 pair.append(moved[at : at + ROWS, :] + 0.5 * gain[at : at + ROWS, :])
                 coll[n, u, part, which] = pair[part]
 
-    def collided(n):
+    def give(n, t, u):
+        q = t * PEERS + u
+
+        @pl.when(q != me)
+        def _():
+            remote(pack_out.at[n, t, u], back.at[n, mine], out_send.at[n], out_recv.at[n], peer_at(q)).start()
+
+        @pl.when(q == me)
+        def _():
+            pltpu.make_async_copy(pack_out.at[n, t, u], back.at[n, mine], out_recv.at[n]).start()
+
+    def finish_mid(n):
+        def tiles_of(u):
+            return [(coll[n, u, part, 1], coll[n, u, part, 1]) for part in range(2)]
+
+        def put_done(u, positive, outs):
+            one, two = swap_halves(outs[0][1], outs[1][1])
+            if positive:
+                pack_out[n, 2, u] = two
+            else:
+                pack_out[n, 1, u] = one
+
+        transport(lambda r: marks[n, r], states, tiles_of, None, put_done, False, True)
+
+        @pl.loop(0, PEERS)
+        def _(d):
+            u = (v + 1 + d) % PEERS
+            give(n, 1 + u // 4, u)
+
+    def finish(n):
         def tiles_of(u):
             return [(coll[n, u, part, 0], coll[n, u, part, 1]) for part in range(2)]
 
-        return tiles_of
-
-    def finish(n):
         def put_done(u, positive, outs):
             one, two = swap_halves(outs[0][1], outs[1][1])
-            pack_out[n, 1, u] = one
-            pack_out[n, 2, u] = two
             ends = swap_halves(outs[0][0], outs[1][0])
             raw = swap_halves(outs[0][2], outs[1][2])
             if positive:
+                pack_out[n, 1, u] = one
                 pack_out[n, 3, u] = ends[1]
                 pack_out[n, 0, u] = raw[0]
                 pack_far[n, u] = raw[1]
             else:
+                pack_out[n, 2, u] = two
                 pack_out[n, 0, u] = ends[0]
                 pack_out[n, 3, u] = raw[1]
                 pack_far[n, u] = raw[0]
 
-        transport(lambda r: marks[n, r], states, collided(n), None, put_done, True, True)
+        transport(lambda r: marks[n, r], states, tiles_of, None, put_done, True, True)
 
         @pl.loop(0, PEERS)
         def _(d):
@@ -454,27 +502,27 @@
             at = (s - turn + total + TURNS * (2 * (u // 4) - 1)) % total + 3 * (1 - u // 4)
             remote(pack_far.at[n, u], far.at[n, mine], far_send.at[n], far_recv.at[n], {"space": at, "vel": u}).start()
 
-        @pl.loop(1, GROUP)
+        @pl.loop(0, 3 * PEERS)
         def _(d):
-            q = (me + d) % GROUP
-            src = pack_out.at[n, q // PEERS, q % PEERS]
-            remote(src, back.at[n, mine], out_send.at[n], out_recv.at[n], peer_at(q)).start()
-
-        pltpu.make_async_copy(pack_out.at[n, turn, v], back.at[n, mine], out_recv.at[n]).start()
+            u = (v + 1 + d) % PEERS
+            k = (turn + d // PEERS) % 3
+            give(n, jnp.where(k == 2, 2 - u // 4, 3 * k), u)
 
     one1 = begin(0)
     work(0, 1)
+    finish_mid(0)
     settle(edges)
     for n in range(CHUNKS):
         lefts = flag_tile([edge[0, 0:1, :], edge[0, 1:2, :], None, None], offset + 2 * n)
         rights = flag_tile([None, None, edge[1, 0:1, :], edge[1, 1:2, :]], offset + 2 * n)
         marks[n, 0] = jnp.broadcast_to(jnp.where(group == 0, 4.0, lefts), (ROWS, PLANE))
         marks[n, 3] = jnp.broadcast_to(jnp.where(group == total // TURNS - 1, 4.0, rights), (ROWS, PLANE))
+    two1 = begin(1)
     settle(one1)
     work(0, 0)
-    two1 = begin(1)
     finish(0)
     work(1, 1)
+    finish_mid(1)
     settle(two1)
     work(1, 0)
     finish(1)
@@ -490,7 +538,7 @@
             turned = fix(at, turned, turn_groups([far[j % 2, 2 * b + j // 2] for j in range(4)]))
         for part in range(2):
             for x in range(2):
-                result[x, at, part * PLANE : (part + 1) * PLANE] = turned[2 * part + x]
+                out[x, at, part * PLANE : (part + 1) * PLANE] = turned[2 * part + x]
 
     def fix_end(keep, order):
         def fix(at, own, near_by):
@@ -532,14 +580,11 @@
         def _(b):
             unpack(b, None)
 
-    last = pltpu.make_async_copy(result, out, own_sem)
-    last.start()
     for n in range(CHUNKS):
         for buf, sem in ((pack_in, in_send), (back, out_send)):
             pltpu.make_async_copy(buf.at[n, 0 : GROUP - 1], buf.at[n, 0 : GROUP - 1], sem.at[n]).wait()
         pltpu.make_async_copy(pack_far.at[n], pack_far.at[n], far_send.at[n]).wait()
     pltpu.make_async_copy(near.at[0:3], near.at[0:3], flag_send.at[0]).wait()
-    last.wait()
 
 
 def build(distribution, cell_flags, kernel_alpha, kernel_beta, kernel_loss, boundary_states):
@@ -556,7 +601,7 @@
         step_kernel,
         out_shape=jax.ShapeDtypeStruct(distribution.shape, f32),
         in_specs=[anywhere] * 7,
-        out_specs=anywhere,
+        out_specs=pl.BlockSpec(memory_space=pltpu.VMEM),
         scratch_shapes=[
             pltpu.VMEM(distribution.shape, f32),
             pltpu.VMEM((2, 128), jnp.int32),
@@ -575,7 +620,6 @@
             room(CHUNKS, GROUP),
             room(CHUNKS, TURNS, PEERS),
             room(CHUNKS, GROUP),
-            pltpu.VMEM(distribution.shape, f32),
         ]
         + [pltpu.VMEM(block, f32)] * 3
         + [pltpu.VMEM(double, f32)] * 2
@@ -597,7 +641,8 @@
             dma((CHUNKS, 2)),
             dma((3,)),
             dma((3,)),
-            dma(()),
+            pltpu.SemaphoreType.REGULAR,
+            pltpu.SemaphoreType.REGULAR,
         ],
         compiler_params=pltpu.CompilerParams(collective_id=0, has_side_effects=True),
     )(distribution, cell_flags, kernel_alpha, kernel_beta, kernel_loss.reshape(1, VEL), boundary_states, jnp.asarray(tables()))

time: 51.3 us -> 47.1 us (0.918)
  Pallas kernels: 49.3 us -> 45.1 us
    pallas_call x1, Pallas kernels: 49.3 us -> 45.1 us  [build(): pl.pallas_call(step_kernel, out_shape=jax.ShapeDtypeStruct(distribution.s...]
where the time goes in v3:
time: 47.1 us; the launch traced here: 46.9 us
  Pallas kernels  45.1 us (96%)
  local copies, waits for them, and re-layouts  1.87 us (4%)
    pallas_call x1, Pallas kernels, build(): pl.pallas_call(step_kernel, out_shape=jax.ShapeDtypeStruct(distribution.s...  45.1 us
    unnamed x1, local copies, waits for them, and re-layouts  1.87 us

profile of v3, /device:TPU:1, one launch (start us, length us, event | category | flops | bytes accessed | tf_op | source)
XLA Modules:
  0.0 46.9 jit_solution(14158026999950871668)
XLA Ops:
  0.0 45.1 %shard_map.73 = f32[2,128,512]{2,1,0:T(8,128)} custom-call(f32[2,128,512]{2,1,0:T(8,128)} %dist_in.1, s32[2,128]{1,0:T(2,128)} %flags_in.1, f32[8,4096]{1,0:T(8,128)} %alpha_in.1, f32[8,4096]{1,0:T(8,128)} %beta_in.1, f32[1,4096]{1,0:T(1,128)} %bitcast.1, f32[2,4096]{1,0:T(2,128)} %states_in.1, bf16[5,256,256]{2,1,0:T(8,128)(2,1)} %constant.2.clone.tab_in), custom_call_target="tpu_custom_call" | custom-call | tf_op jit(solution)/shard_map/pallas_call | solution.py:600
  45.1 1.9 %copy.9 = f32[2,128,512]{2,1,0:T(8,128)} copy(f32[2,128,512]{2,1,0:T(8,128)} %shard_map.73) | data formatting | bytes 1048576

commit v4 on v1

--- a/solution.py
+++ b/solution.py
@@ -18,6 +18,7 @@
 GROUP = TURNS * PEERS
 ROWS = 8
 CHUNKS = 2
+GATE_TURN, GATE_PEER = 1, 2
 MESH = pl.DeviceIdType.MESH
 f32 = jnp.float32
 bf16 = jnp.bfloat16
@@ -272,9 +273,9 @@
 def step_kernel(
     dist_in, flags_in, alpha_in, beta_in, loss_in, states_in, tab_in, out,
     dist, flags, alpha, beta, loss, states, tab, load_sem,
-    pack_in, recv, left1, right1, coll, edge_out, left2, right2, pack_out, back, result,
+    pack_in, recv, left1, right1, coll, edge_out, left2, right2, pack_out, back,
     moved, spec, modes, first, second, gain, packed, filters, near, edge, marks,
-    in_send, in_recv, out_send, out_recv, halo_send, halo_recv, flag_send, flag_recv, own_sem,
+    in_send, in_recv, out_send, out_recv, halo_send, halo_recv, flag_send, flag_recv, gate_sem, ready_sem,
 ):
     s, v = lax.axis_index("space"), lax.axis_index("vel")
     total = lax.axis_size("space")
@@ -283,7 +284,7 @@
     me = turn * PEERS + v
 
     def mirror(peer):
-        return (3 - peer // 2) * 2 + peer % 2
+        return (peer + PEERS // 2) % PEERS
 
     def block_of(t, peer):
         return (peer + upper * (mirror(peer) - peer)) * TURNS + t
@@ -301,18 +302,27 @@
             [(dist_in, dist), (flags_in, flags), (alpha_in, alpha), (beta_in, beta), (loss_in, loss), (states_in, states), (tab_in, tab)]
         )
     ]
-    for copy in loads:
-        copy.start()
+    loads[0].start()
     barrier = pltpu.get_barrier_semaphore()
 
     @pl.loop(1, GROUP)
     def _(d):
         pl.semaphore_signal(barrier, inc=1, device_id=peer_at((me + d) % GROUP), device_id_type=MESH)
 
-    for at in (left, right):
-        pl.semaphore_signal(barrier, inc=1, device_id=at, device_id_type=MESH)
+    gate = jnp.logical_and(turn == GATE_TURN, v == GATE_PEER)
+
+    def next_gate(semaphore):
+        for step in (TURNS, total - TURNS):
+            at = {"space": (s + step) % total, "vel": v}
+            pl.semaphore_signal(semaphore, inc=1, device_id=at, device_id_type=MESH)
+
+    @pl.when(gate)
+    def _():
+        next_gate(barrier)
 
     loads[0].wait()
+    for copy in loads[1:]:
+        copy.start()
 
     @pl.loop(0, GROUP // 2)
     def _(b):
@@ -321,9 +331,8 @@
         for j in range(4):
             pack_in[j % 2, 2 * b + j // 2] = turned[j]
 
-    for copy in loads[1:]:
-        copy.wait()
-    pl.semaphore_wait(barrier, GROUP + 1)
+    loads[1].wait()
+    pl.semaphore_wait(barrier, jnp.where(gate, GROUP + 1, GROUP - 1))
 
     def remote(src, dst, send, rec, at):
         return pltpu.make_async_remote_copy(
@@ -335,15 +344,30 @@
         remote(flags, near.at[turn], flag_send.at[0], flag_recv.at[0], at).start()
     pltpu.make_async_copy(flags, near.at[turn], flag_recv.at[0]).start()
 
+    upward = jnp.logical_and(turn == TURNS - 1, v >= PEERS // 2)
+    downward = jnp.logical_and(turn == 0, v < PEERS // 2)
+    kind = jnp.where(upward, 0, jnp.where(downward, 1, 2))
     for n in range(CHUNKS):
 
         @pl.loop(1, GROUP)
         def _(d):
             q = (me + d) % GROUP
             src = pack_in.at[n, block_of(q // PEERS, q % PEERS)]
-            remote(src, recv.at[n, turn, v], in_send.at[n], in_recv.at[n], peer_at(q)).start()
-
-        pltpu.make_async_copy(pack_in.at[n, mine], recv.at[n, turn, v], in_recv.at[n]).start()
+            remote(src, recv.at[n, turn, v], in_send.at[n], in_recv.at[n, kind], peer_at(q)).start()
+
+        pltpu.make_async_copy(pack_in.at[n, mine], recv.at[n, turn, v], in_recv.at[n, kind]).start()
+
+    @pl.when(gate)
+    def _():
+        next_gate(gate_sem)
+        pl.semaphore_wait(gate_sem, 2)
+
+        @pl.loop(1, GROUP)
+        def _(d):
+            pl.semaphore_signal(ready_sem, inc=1, device_id=peer_at((me + d) % GROUP), device_id_type=MESH)
+
+    for copy in loads[2:]:
+        copy.wait()
 
     def pick(rest):
         got = jnp.zeros(rest.shape, f32)
@@ -367,6 +391,10 @@
                 filters[f, k, part] = jnp.broadcast_to(row, (ROWS, 128))
 
     pltpu.make_async_copy(near, near, flag_recv.at[0]).wait()
+    @pl.when(jnp.logical_not(gate))
+    def _():
+        pl.semaphore_wait(ready_sem, 1)
+
     edges = [
         remote(near.at[3], edge.at[0], flag_send.at[1], flag_recv.at[1], right),
         remote(near.at[0], edge.at[1], flag_send.at[2], flag_recv.at[2], left),
@@ -379,20 +407,32 @@
             rows = [near[pair[r // 2], r % 2 : r % 2 + 1, :] for r in range(4)]
             marks[n, at] = jnp.broadcast_to(flag_tile(rows, offset + 2 * n), (ROWS, PLANE))
 
-    def exchange(at, ups, downs, ups_dst, downs_dst):
-        one = remote(ups, ups_dst, halo_send.at[at, 0], halo_recv.at[at, 0], right)
-        two = remote(downs, downs_dst, halo_send.at[at, 1], halo_recv.at[at, 1], left)
-        one.start()
-        two.start()
-        return [one, two]
-
     def settle(copies):
         for copy in copies:
             copy.wait()
 
+    def exchange(at, ends, before):
+        copies = []
+        for way, (src, dst, to) in enumerate(ends):
+            before(way, src)
+            copies.append(remote(src, dst, halo_send.at[at, way], halo_recv.at[at, way], to))
+            copies[way].start()
+        return copies
+
     def begin(n):
-        pltpu.make_async_copy(recv.at[n], recv.at[n], in_recv.at[n]).wait()
-        return exchange(n, recv.at[n, 3, 4:8], recv.at[n, 0, 0:4], left1.at[n], right1.at[n])
+        def landed(way, src):
+            pltpu.make_async_copy(src, src, in_recv.at[n, way]).wait()
+
+        ends = ((recv.at[n, 3, 4:8], left1.at[n], right), (recv.at[n, 0, 0:4], right1.at[n], left))
+        return exchange(n, ends, landed)
+
+    def pass_on(n):
+        ends = ((edge_out.at[n, 0], left2.at[n], right), (edge_out.at[n, 1], right2.at[n], left))
+        return exchange(CHUNKS + n, ends, lambda way, src: None)
+
+    def rest_of(n):
+        rest = recv.at[n, 0:3]
+        pltpu.make_async_copy(rest, rest, in_recv.at[n, 2]).wait()
 
     def work(n, which):
         def tiles_of(u):
@@ -421,9 +461,6 @@
             if which == 0 and u >= 4:
                 edge_out[n, 0, u - 4] = swap_halves(*pair)[1]
 
-    def pass_on(n):
-        return exchange(CHUNKS + n, edge_out.at[n, 0], edge_out.at[n, 1], left2.at[n], right2.at[n])
-
     def give(n, t, u):
         q = t * PEERS + u
 
@@ -435,7 +472,25 @@
         def _():
             pltpu.make_async_copy(pack_out.at[n, t, u], back.at[n, mine], out_recv.at[n]).start()
 
-    def collided(n):
+    def finish_mid(n):
+        def tiles_of(u):
+            return [(coll[n, u, part, 1], coll[n, u, part, 1]) for part in range(2)]
+
+        def put_done(u, positive, outs):
+            one, two = swap_halves(outs[0][1], outs[1][1])
+            if positive:
+                pack_out[n, 2, u] = two
+            else:
+                pack_out[n, 1, u] = one
+
+        transport(lambda r: marks[n, r], states, tiles_of, None, put_done, False, True)
+
+        @pl.loop(0, PEERS)
+        def _(d):
+            u = (v + 1 + d) % PEERS
+            give(n, 1 + u // 4, u)
+
+    def tiles_done(n):
         def tiles_of(u):
             return [(coll[n, u, part, 0], coll[n, u, part, 1]) for part in range(2)]
 
@@ -444,20 +499,21 @@
     def finish_most(n):
         def put_done(u, positive, outs):
             one, two = swap_halves(outs[0][1], outs[1][1])
-            pack_out[n, 1, u] = one
-            pack_out[n, 2, u] = two
             ends = swap_halves(outs[0][0], outs[1][0])
             if positive:
+                pack_out[n, 1, u] = one
                 pack_out[n, 3, u] = ends[1]
             else:
+                pack_out[n, 2, u] = two
                 pack_out[n, 0, u] = ends[0]
 
-        transport(lambda r: marks[n, r], states, collided(n), None, put_done, True, True)
-
-        @pl.loop(0, 3 * PEERS)
+        transport(lambda r: marks[n, r], states, tiles_done(n), None, put_done, True, True)
+
+        @pl.loop(0, 2 * PEERS)
         def _(d):
             u = (v + 1 + d) % PEERS
-            give(n, (turn + d // PEERS) % 3 + u // 4, u)
+            k = (turn + d // PEERS) % 2
+            give(n, (2 - u // 4) * k + (3 * (u // 4)) * (1 - k), u)
 
     def finish_rest(n):
         def halo_of(u, positive):
@@ -470,7 +526,7 @@
             else:
                 pack_out[n, 3, u] = ends[1]
 
-        transport(lambda r: marks[n, r], states, collided(n), halo_of, put_done, True, False)
+        transport(lambda r: marks[n, r], states, tiles_done(n), halo_of, put_done, True, False)
 
         @pl.loop(0, PEERS)
         def _(d):
@@ -478,25 +534,29 @@
             give(n, 3 - 3 * (u // 4), u)
 
     one1 = begin(0)
+    rest_of(0)
     work(0, 1)
+    finish_mid(0)
     settle(edges)
     for n in range(CHUNKS):
         lefts = flag_tile([edge[0, 0:1, :], edge[0, 1:2, :], None, None], offset + 2 * n)
         rights = flag_tile([None, None, edge[1, 0:1, :], edge[1, 1:2, :]], offset + 2 * n)
         marks[n, 0] = jnp.broadcast_to(jnp.where(group == 0, 4.0, lefts), (ROWS, PLANE))
         marks[n, 3] = jnp.broadcast_to(jnp.where(group == total // TURNS - 1, 4.0, rights), (ROWS, PLANE))
+    two1 = begin(1)
+    rest_of(1)
+    work(1, 1)
+    finish_mid(1)
     settle(one1)
     work(0, 0)
     one2 = pass_on(0)
-    two1 = begin(1)
     finish_most(0)
-    work(1, 1)
-    settle(one2)
-    finish_rest(0)
     settle(two1)
     work(1, 0)
     two2 = pass_on(1)
     finish_most(1)
+    settle(one2)
+    finish_rest(0)
     settle(two2)
     finish_rest(1)
     for n in range(CHUNKS):
@@ -508,15 +568,12 @@
         turned = turn_groups([back[j % 2, 2 * b + j // 2] for j in range(4)])
         for part in range(2):
             for x in range(2):
-                result[x, at, part * PLANE : (part + 1) * PLANE] = turned[2 * part + x]
-
-    last = pltpu.make_async_copy(result, out, own_sem)
-    last.start()
+                out[x, at, part * PLANE : (part + 1) * PLANE] = turned[2 * part + x]
+
     for n in range(CHUNKS):
         for buf, sem in ((pack_in, in_send), (back, out_send)):
             pltpu.make_async_copy(buf.at[n, 0 : GROUP - 1], buf.at[n, 0 : GROUP - 1], sem.at[n]).wait()
     pltpu.make_async_copy(near.at[0:3], near.at[0:3], flag_send.at[0]).wait()
-    last.wait()
 
 
 def build(distribution, cell_flags, kernel_alpha, kernel_beta, kernel_loss, boundary_states):
@@ -533,7 +590,7 @@
         step_kernel,
         out_shape=jax.ShapeDtypeStruct(distribution.shape, f32),
         in_specs=[anywhere] * 7,
-        out_specs=anywhere,
+        out_specs=pl.BlockSpec(memory_space=pltpu.VMEM),
         scratch_shapes=[
             pltpu.VMEM(distribution.shape, f32),
             pltpu.VMEM((2, 128), jnp.int32),
@@ -553,7 +610,6 @@
             room(CHUNKS, PEERS // 2),
             room(CHUNKS, TURNS, PEERS),
             room(CHUNKS, GROUP),
-            pltpu.VMEM(distribution.shape, f32),
         ]
         + [pltpu.VMEM(block, f32)] * 3
         + [pltpu.VMEM(double, f32)] * 2
@@ -565,14 +621,15 @@
             pltpu.VMEM((2, 2, 128), jnp.int32),
             room(CHUNKS, 4),
             dma((CHUNKS,)),
-            dma((CHUNKS,)),
+            dma((CHUNKS, 3)),
             dma((CHUNKS,)),
             dma((CHUNKS,)),
             dma((2 * CHUNKS, 2)),
             dma((2 * CHUNKS, 2)),
             dma((3,)),
             dma((3,)),
-            dma(()),
+            pltpu.SemaphoreType.REGULAR,
+            pltpu.SemaphoreType.REGULAR,
         ],
         compiler_params=pltpu.CompilerParams(collective_id=0, has_side_effects=True),
     )(distribution, cell_flags, kernel_alpha, kernel_beta, kernel_loss.reshape(1, VEL), boundary_states, jnp.asarray(tables()))

time: 53.4 us -> 45.7 us (0.86)
  Pallas kernels: 51.4 us -> 43.6 us
    pallas_call x1, Pallas kernels: 51.4 us -> 43.6 us  [build(): pl.pallas_call(step_kernel, out_shape=jax.ShapeDtypeStruct(distribution.s...]
where the time goes in v4:
time: 45.7 us; the launch traced here: 45.5 us
  Pallas kernels  43.6 us (95%)
  local copies, waits for them, and re-layouts  1.87 us (4%)
    pallas_call x1, Pallas kernels, build(): pl.pallas_call(step_kernel, out_shape=jax.ShapeDtypeStruct(distribution.s...  43.6 us
    unnamed x1, local copies, waits for them, and re-layouts  1.87 us

profile of v4, /device:TPU:25, one launch (start us, length us, event | category | flops | bytes accessed | tf_op | source)
XLA Modules:
  0.0 45.5 jit_solution(4120261889278798688)
XLA Ops:
  0.0 43.6 %shard_map.73 = f32[2,128,512]{2,1,0:T(8,128)} custom-call(f32[2,128,512]{2,1,0:T(8,128)} %dist_in.1, s32[2,128]{1,0:T(2,128)} %flags_in.1, f32[8,4096]{1,0:T(8,128)} %alpha_in.1, f32[8,4096]{1,0:T(8,128)} %beta_in.1, f32[1,4096]{1,0:T(1,128)} %bitcast.1, f32[2,4096]{1,0:T(2,128)} %states_in.1, bf16[5,256,256]{2,1,0:T(8,128)(2,1)} %constant.2.clone.tab_in), custom_call_target="tpu_custom_call" | custom-call | tf_op jit(solution)/shard_map/pallas_call | solution.py:589
  43.6 1.9 %copy.9 = f32[2,128,512]{2,1,0:T(8,128)} copy(f32[2,128,512]{2,1,0:T(8,128)} %shard_map.73) | data formatting | bytes 1048576

commit v5 on v4

--- a/solution.py
+++ b/solution.py
@@ -235,15 +235,20 @@
         put(modes, k, done[k])
 
     def filtered(index, target, base):
-        z = [piece(modes, k) for k in range(VG)]
-        w = []
-        for k in range(VG):
+        def weighed(k):
             near, far = filters[index, k, 0], filters[index, k, 1]
-            twin = z[-k % VG]
-            w.append((near * z[k][0] + far * twin[0], near * z[k][1] - far * twin[1]))
-        done = line_inverse(w)
-        for k in range(VG):
-            put(target, k, done[k], base)
+            (re, im), (twin_re, twin_im) = piece(modes, k), piece(modes, -k % VG)
+            return im * near - far * twin_im, re * near + far * twin_re
+
+        for b in range(4):
+            group = four_points([weighed(4 * a + b) for a in range(4)])
+            for k in range(4):
+                put(target, 4 * b + k, times_root(*group[k], b * k), base)
+        for k in range(4):
+            group = four_points([piece(target, 4 * b + k, base) for b in range(4)])
+            for m in range(4):
+                re, im = group[m]
+                put(target, k + 4 * m, (im, re), base)
 
     def both(p, target):
         filtered(p, target, 0)

time: 45.7 us -> 45.3 us (level)
  no operation moved by 1% of the time
where the time goes in v5:
time: 45.3 us; the launch traced here: 45.1 us
  Pallas kernels  43.2 us (95%)
  local copies, waits for them, and re-layouts  1.87 us (4%)
    pallas_call x1, Pallas kernels, build(): pl.pallas_call(step_kernel, out_shape=jax.ShapeDtypeStruct(distribution.s...  43.2 us
    unnamed x1, local copies, waits for them, and re-layouts  1.87 us

profile of v5, /device:TPU:25, one launch (start us, length us, event | category | flops | bytes accessed | tf_op | source)
XLA Modules:
  0.0 45.1 jit_solution(6422975463574098933)
XLA Ops:
  0.0 43.2 %shard_map.73 = f32[2,128,512]{2,1,0:T(8,128)} custom-call(f32[2,128,512]{2,1,0:T(8,128)} %dist_in.1, s32[2,128]{1,0:T(2,128)} %flags_in.1, f32[8,4096]{1,0:T(8,128)} %alpha_in.1, f32[8,4096]{1,0:T(8,128)} %beta_in.1, f32[1,4096]{1,0:T(1,128)} %bitcast.1, f32[2,4096]{1,0:T(2,128)} %states_in.1, bf16[5,256,256]{2,1,0:T(8,128)(2,1)} %constant.2.clone.tab_in), custom_call_target="tpu_custom_call" | custom-call | tf_op jit(solution)/shard_map/pallas_call | solution.py:594
  43.2 1.9 %copy.9 = f32[2,128,512]{2,1,0:T(8,128)} copy(f32[2,128,512]{2,1,0:T(8,128)} %shard_map.73) | data formatting | bytes 1048576

commit v6 on v5

--- a/solution.py
+++ b/solution.py
@@ -304,10 +304,14 @@
     loads = [
         pltpu.make_async_copy(src, dst, load_sem.at[i])
         for i, (src, dst) in enumerate(
-            [(dist_in, dist), (flags_in, flags), (alpha_in, alpha), (beta_in, beta), (loss_in, loss), (states_in, states), (tab_in, tab)]
+            [(flags_in, flags), (alpha_in, alpha), (beta_in, beta), (loss_in, loss), (states_in, states), (tab_in, tab)]
         )
     ]
-    loads[0].start()
+    quarters = []
+    for part in range(4):
+        at = pl.ds(part * 32, 32)
+        quarters.append(pltpu.make_async_copy(dist_in.at[:, at, :], dist.at[:, at, :], load_sem.at[6 + part]))
+        quarters[part].start()
     barrier = pltpu.get_barrier_semaphore()
 
     @pl.loop(1, GROUP)
@@ -325,18 +329,20 @@
     def _():
         next_gate(barrier)
 
-    loads[0].wait()
-    for copy in loads[1:]:
+    for copy in loads:
         copy.start()
 
-    @pl.loop(0, GROUP // 2)
-    def _(b):
+    def pack_block(b):
         at = pl.ds(pl.multiple_of(b * ROWS, ROWS), ROWS)
         turned = turn_groups([dist[x, at, part * PLANE : (part + 1) * PLANE] for part in range(2) for x in range(2)])
         for j in range(4):
             pack_in[j % 2, 2 * b + j // 2] = turned[j]
 
-    loads[1].wait()
+    for part in range(4):
+        quarters[part].wait()
+        pl.loop(4 * part, 4 * part + 4)(pack_block)
+
+    loads[0].wait()
     pl.semaphore_wait(barrier, jnp.where(gate, GROUP + 1, GROUP - 1))
 
     def remote(src, dst, send, rec, at):
@@ -371,7 +377,7 @@
         def _(d):
             pl.semaphore_signal(ready_sem, inc=1, device_id=peer_at((me + d) % GROUP), device_id_type=MESH)
 
-    for copy in loads[2:]:
+    for copy in loads[1:]:
         copy.wait()
 
     def pick(rest):
@@ -604,7 +610,7 @@
             pltpu.VMEM((1, VEL), f32),
             pltpu.VMEM((2, VEL), f32),
             pltpu.VMEM((5, PLANE, PLANE), bf16),
-            dma((7,)),
+            dma((10,)),
             room(CHUNKS, GROUP),
             room(CHUNKS, TURNS, PEERS),
             room(CHUNKS, PEERS // 2),

time: 45.3 us -> 45.4 us (level)
  no operation moved by 1% of the time
where the time goes in v6:
time: 45.4 us; the launch traced here: 45.2 us
  Pallas kernels  43.3 us (95%)
  local copies, waits for them, and re-layouts  1.87 us (4%)
    pallas_call x1, Pallas kernels, build(): pl.pallas_call(step_kernel, out_shape=jax.ShapeDtypeStruct(distribution.s...  43.3 us
    unnamed x1, local copies, waits for them, and re-layouts  1.87 us

profile of v6, /device:TPU:25, one launch (start us, length us, event | category | flops | bytes accessed | tf_op | source)
XLA Modules:
  0.0 45.2 jit_solution(5275334248322845541)
XLA Ops:
  0.0 43.3 %shard_map.73 = f32[2,128,512]{2,1,0:T(8,128)} custom-call(f32[2,128,512]{2,1,0:T(8,128)} %dist_in.1, s32[2,128]{1,0:T(2,128)} %flags_in.1, f32[8,4096]{1,0:T(8,128)} %alpha_in.1, f32[8,4096]{1,0:T(8,128)} %beta_in.1, f32[1,4096]{1,0:T(1,128)} %bitcast.1, f32[2,4096]{1,0:T(2,128)} %states_in.1, bf16[5,256,256]{2,1,0:T(8,128)(2,1)} %constant.2.clone.tab_in), custom_call_target="tpu_custom_call" | custom-call | tf_op jit(solution)/shard_map/pallas_call | solution.py:600
  43.3 1.9 %copy.9 = f32[2,128,512]{2,1,0:T(8,128)} copy(f32[2,128,512]{2,1,0:T(8,128)} %shard_map.73) | data formatting | bytes 1048576
